TPU v7x, 32 devices: a whole 2x2x4 slice. The times are simulated.
32 devices in a mesh: paths: 2 (over y), tm: 16 (over z, x, core).
Axes of the slice: x: 2, y: 2, z: 4, core: 2. Of those that a mesh axis runs over, the one named last changes fastest.
Arguments:
- independent_disturbances: bfloat16 [1024, 8, 1024], P('tm', 'paths'), may hold values from -6 to 6
- starting_driver_values: float32 [8, 1024], P('paths'), may hold values from -6 to 6
- correlation_mixer: bfloat16 [1024, 1024], P('paths'), may hold values from -0.1875 to 0.1875
- log_persistence: float32 [1024], replicated, may hold values from -0.034 to 0
- regime_multiplier: float32 [1024], P('tm'), may hold values from 0.5 to 1
- payoff_per_unit_table: bfloat16 [1024, 128], replicated, may hold values from -0.1875 to 0.1875
- short_yield_coefficients: bfloat16 [1024], replicated, may hold values from -0.1875 to 0.1875
Outputs:
- values: float32 [8, 128], P('paths')
All inputs are finite; a program needn't handle non-finite values.
Results may differ from a plain program's by a relative error of at most 0.0004.
Values may be sent and summed in bfloat16 or wider, within the bound.
No kernel may reach another device: no remote copies, remote signals or barrier semaphores. Data moves between devices by JAX's collectives and lax.ppermute only.
A program may use at most 64 MiB of HBM per device.

v0:
```python
import jax
import jax.numpy as jnp
from jax import lax
from jax.sharding import PartitionSpec as P


def entering(part, axis, combine, identity):
    place = lax.axis_index(axis)
    gathered = jax.tree.map(lambda a: lax.all_gather(a, axis), part)
    state = jax.tree.map(lambda a, e: jnp.zeros_like(a) + jnp.asarray(e, a.dtype), part, identity)

    def one(turn, state):
        return combine(
            state, jax.tree.map(lambda a: lax.dynamic_index_in_dim(a, turn, 0, False), gathered)
        )

    return lax.fori_loop(0, place, one, state)


def local(
    independent_disturbances,
    starting_driver_values,
    correlation_mixer,
    log_persistence,
    regime_multiplier,
    payoff_per_unit_table,
    short_yield_coefficients,
):
    slab_days, group_paths, driver_value_history = independent_disturbances.shape
    where_now = lax.axis_index("tm")
    correlated_disturbances = jnp.einsum(
        "spf,fg->spg",
        independent_disturbances,
        lax.all_gather(correlation_mixer, "paths", axis=0, tiled=True),
        preferred_element_type=jnp.float32,
    )
    persistence_multiplier = jnp.exp(log_persistence)
    vol = jnp.sqrt(-jnp.expm1(2.0 * log_persistence))
    leading_element = jnp.where(
        where_now == 0, starting_driver_values, jnp.zeros_like(starting_driver_values)
    )

    def propagate_one_day(carry, operand_tensors):
        state, decay = carry
        random_normal_sample, regime_multiplier_today = operand_tensors
        driver_value_now = persistence_multiplier * regime_multiplier_today
        state = driver_value_now * state + vol * random_normal_sample
        decay = decay * driver_value_now
        return ((state, decay), (state, decay))

    (state, decay), (local_states, local_decays) = lax.scan(
        propagate_one_day,
        (leading_element, jnp.ones((driver_value_history,), jnp.float32)),
        (correlated_disturbances, regime_multiplier),
    )

    def chain(earlier, later):
        return (earlier[0] * later[0], later[0][None, :] * earlier[1] + later[1])

    identity = (
        jnp.ones((driver_value_history,), jnp.float32),
        jnp.zeros((group_paths, driver_value_history), jnp.float32),
    )
    carried = entering((decay, state), "tm", chain, identity)
    driver_trajectory = local_states + local_decays[:, None, :] * carried[1][None, :, :]
    scenario = driver_trajectory.astype(jnp.bfloat16)
    horizon_days = slab_days * lax.axis_size("tm")
    cash = jnp.einsum(
        "tpf,fk->tpk", scenario, payoff_per_unit_table, preferred_element_type=jnp.float32
    )
    rate = 0.03 + 0.3 * jnp.einsum(
        "tpf,f->tp", scenario, short_yield_coefficients, preferred_element_type=jnp.float32
    )
    running = jnp.cumsum(rate, axis=0)

    def added(earlier, later):
        return earlier + later

    before = entering(running[-1], "tm", added, jnp.zeros((group_paths,), jnp.float32))
    discount = jnp.exp(-(1.0 / 256.0) * (before[None, :] + running))
    partial_sum = jnp.sum(discount[:, :, None] * cash, axis=0) / horizon_days
    return lax.psum(partial_sum, "tm")


def solution(mesh):
    in_specs = (P("tm", "paths", None), P("paths", None), P("paths", None), P(), P("tm"), P(), P())
    out_specs = P("paths", None)
    return jax.shard_map(local, mesh=mesh, in_specs=in_specs, out_specs=out_specs, check_vma=False)
```

profile of v0, /device:TPU:0, one launch (start us, length us, event | category | flops | bytes accessed | tf_op | source)
XLA Modules:
  0.0 240.3 jit_solution(8618859963692799601)
XLA Ops:
  6.5 0.7 all-gather.6.cloned.1.call-update
  7.3 0.7 reshape.30
  8.0 0.7 negate_sqrt_fusion
  8.7 0.7 broadcast_select_fusion
  9.4 35.3 %all-gather.6.cloned.1.call-done = bf16[1024,1024]{1,0:T(8,128)(2,1)} async-done(((bf16[512,1024]{1,0:T(8,128)(2,1)}), bf16[1024,1024]{1,0:T(8,128)(2,1)}) %all-gather.6.cloned.1.call-update) | async-done | bytes 2097168 | tf_op jit(solution)/shard_map/all_gather | solution.py:34
  44.7 2.5 %fusion.2 = f32[64,4,1024]{2,0,1:T(8,128)S(1)} fusion(bf16[1024,1024]{1,0:T(8,128)(2,1)} %all-gather.6.cloned.1.call-done, bf16[64,4,1024]{2,1,0:T(4,128)(2,1)} %param.13), kind=kOutput, calls=%fused_computation.10 | convolution fusion | flops 536870912 | bytes 3670016 | tf_op jit(solution)/shard_map/spf,fg->spg/dot_general | solution.py:31
  47.2 95.1 %while.41 = (s32[]{:T(128)}, f32[4,1024]{1,0:T(4,128)S(1)}, f32[1024]{0:T(1024)S(1)}, f32[64,4,1024]{2,1,0:T(4,128)S(1)}, f32[64,1024]{1,0:T(8,128)S(1)}, /*inde...) while((s32[]{:T(128)}, f32[4,1024]{1,0:T(4,128)S(1)}, ...), condition=%wide.region_1.2_spmd.clone, body=%wide.region_0.1_spmd.clone.sunk | while | flops 15363 | bytes 131219 | solution.py:51
  47.3 0.7 dynamic_slice.37
  48.7 0.7 dynamic_slice.37
  50.2 0.7 dynamic_slice.37
  51.7 0.7 dynamic_slice.37
  53.2 0.7 dynamic_slice.37
  54.7 0.7 dynamic_slice.37
  56.2 0.7 dynamic_slice.37
  57.7 0.7 dynamic_slice.37
  59.1 0.7 dynamic_slice.37
  60.6 0.7 dynamic_slice.37
  62.1 0.7 dynamic_slice.37
  63.6 0.7 dynamic_slice.37
  65.1 0.7 dynamic_slice.37
  66.6 0.7 dynamic_slice.37
  68.1 0.7 dynamic_slice.37
  69.5 0.7 dynamic_slice.37
  71.0 0.7 dynamic_slice.37
  72.5 0.7 dynamic_slice.37
  74.0 0.7 dynamic_slice.37
  75.5 0.7 dynamic_slice.37
  77.0 0.7 dynamic_slice.37
  78.5 0.7 dynamic_slice.37
  79.9 0.7 dynamic_slice.37
  81.4 0.7 dynamic_slice.37
  82.9 0.7 dynamic_slice.37
  84.4 0.7 dynamic_slice.37
  85.9 0.7 dynamic_slice.37
  87.4 0.7 dynamic_slice.37
  88.9 0.7 dynamic_slice.37
  90.3 0.7 dynamic_slice.37
  91.8 0.7 dynamic_slice.37
  93.3 0.7 dynamic_slice.37
  94.8 0.7 dynamic_slice.37
  96.3 0.7 dynamic_slice.37
  97.8 0.7 dynamic_slice.37
  99.3 0.7 dynamic_slice.37
  100.7 0.7 dynamic_slice.37
  102.2 0.7 dynamic_slice.37
  103.7 0.7 dynamic_slice.37
  105.2 0.7 dynamic_slice.37
  106.7 0.7 dynamic_slice.37
  108.2 0.7 dynamic_slice.37
  109.7 0.7 dynamic_slice.37
  111.1 0.7 dynamic_slice.37
  112.6 0.7 dynamic_slice.37
  114.1 0.7 dynamic_slice.37
  115.6 0.7 dynamic_slice.37
  117.1 0.7 dynamic_slice.37
  118.6 0.7 dynamic_slice.37
  120.1 0.7 dynamic_slice.37
  121.5 0.7 dynamic_slice.37
  123.0 0.7 dynamic_slice.37
  124.5 0.7 dynamic_slice.37
  142.3 22.0 %all-gather.2 = f32[16,4,1024]{2,1,0:T(4,128)S(1)} all-gather(f32[1,4,1024]{2,1,0:T(4,128)S(1)} %bitcast.43), channel_id=3, replica_groups=mesh['paths'=2,'tm'=16] {'tm'}, dimensions={0}, use_global_device_ids=true | all-gather | bytes 278528 | tf_op jit(solution)/shard_map/all_gather | solution.py:9
  164.4 17.6 %all-gather = f32[16384]{0:T(1024)S(1)} all-gather(f32[1024]{0:T(1024)S(1)} %get-tuple-element.124), channel_id=2, replica_groups=mesh['paths'=2,'tm'=16] {'tm'}, dimensions={0}, use_global_device_ids=true | all-gather | bytes 69632 | tf_op jit(solution)/shard_map/all_gather | solution.py:9
  182.9 19.7 %all-gather.3 = f32[16,1,4]{2,1,0:T(1,128)S(1)} all-gather(f32[1,1,4]{2,1,0:T(1,128)S(1)} %slice_bitcast_fusion), channel_id=1, replica_groups=mesh['paths'=2,'tm'=16] {'tm'}, dimensions={0}, use_global_device_ids=true | all-gather | bytes 272 | tf_op jit(solution)/shard_map/all_gather | solution.py:9
  203.1 30.4 %psum.7 = f32[4,128]{1,0:T(4,128)} all-reduce(f32[4,128]{1,0:T(4,128)S(1)} %broadcast_multiply_fusion.1), channel_id=1, replica_groups=mesh['paths'=2,'tm'=16] {'tm'}, use_global_device_ids=true, to_apply=%region_8.9 | all-reduce | flops 512 | bytes 4096 | tf_op jit(solution)/shard_map/psum | solution.py:82
  (290 shorter events, 59.3 us)
Async XLA Ops:
  6.5 196.2 %copy-start = (bf16[1024,128]{1,0:T(8,128)(2,1)S(1)}, bf16[1024,128]{1,0:T(8,128)(2,1)}, u32[]{:S(2)}) copy-start(bf16[1024,128]{1,0:T(8,128)(2,1)} %param.18) | copy-start | bytes 786436
  6.5 38.2 %all-gather.6.cloned.1.call-start = ((), (), s32[]{:S(2)}) async-start(), calls=%async_computation | async-start | bytes 3145728 | tf_op jit(solution)/shard_map/all_gather | solution.py:34
  7.3 40.0 %copy-start.1 = (f32[64]{0:T(128)S(1)}, f32[64]{0:T(128)}, u32[]{:S(2)}) copy-start(f32[64]{0:T(128)} %param.17) | copy-start | bytes 772
Sparse Core Ops, SparseCore 0:
  8.9 35.8 all-gather.5
where the time goes:
time: 241 us; the launch traced here: 240 us
  blocking collectives  89.8 us (37%)
  local copies, waits for them, and re-layouts  51 us (21%)
  other arithmetic  44.2 us (18%)
  waiting for transfers between devices  36 us (15%)
  between operations  13.5 us (6%)
  matrix products  3.15 us (1%)
  loops' own time  2.71 us (1%)
    all_gather x3, blocking collectives, entering(): gathered = jax.tree.map(lambda a: lax.all_gather(a, axis), part)  59.4 us
    dynamic_slice x128, local copies, waits for them, and re-layouts, local(): lax.scan(propagate_one_day, (leading_element, jnp.ones((driver_value_hist...  43 us
    mul x64, other arithmetic, propagate_one_day(): decay = decay * driver_value_now  40.6 us
    all_gather x1, waiting for transfers between devices, local(): lax.all_gather(correlation_mixer, 'paths', axis=0, tiled=True)  35.3 us
    psum x1, blocking collectives, local(): return lax.psum(partial_sum, 'tm')  30.4 us
    dynamic_update_slice x64, local copies, waits for them, and re-layouts, local(): lax.scan(propagate_one_day, (leading_element, jnp.ones((driver_value_hist...  7.04 us
  transfers between devices with their start and end apart: 1, of which 1 were waited for; matrix products, arithmetic and copies ran while one was open for 1% of the time, Pallas kernels for 0%

commit v1 on v0

--- a/solution.py
+++ b/solution.py
@@ -2,6 +2,12 @@
 import jax.numpy as jnp
 from jax import lax
 from jax.sharding import PartitionSpec as P
+
+
+def summed_here(x, mesh_axis):
+    parts = lax.all_gather(x, mesh_axis, axis=0, tiled=False)
+    total = parts.sum(axis=0)
+    return total
 
 
 def entering(part, axis, combine, identity):
@@ -79,7 +85,7 @@
     before = entering(running[-1], "tm", added, jnp.zeros((group_paths,), jnp.float32))
     discount = jnp.exp(-(1.0 / 256.0) * (before[None, :] + running))
     partial_sum = jnp.sum(discount[:, :, None] * cash, axis=0) / horizon_days
-    return lax.psum(partial_sum, "tm")
+    return summed_here(partial_sum, "tm")
 
 
 def solution(mesh):

time: 241 us -> 229 us (0.950)
  blocking collectives: 89.8 us -> 76.9 us
    psum x1 -> x0, blocking collectives: 30.4 us -> none  [local(): return lax.psum(partial_sum, 'tm')]
    all_gather x0 -> x1, blocking collectives: none -> 17.5 us  [summed_here(): parts = lax.all_gather(x, mesh_axis, axis=0, tiled=False)]
where the time goes in v1:
time: 229 us; the launch traced here: 228 us
  blocking collectives  76.9 us (34%)
  local copies, waits for them, and re-layouts  51 us (22%)
  other arithmetic  44.8 us (20%)
  waiting for transfers between devices  36 us (16%)
  between operations  13.5 us (6%)
  matrix products  3.15 us (1%)
  loops' own time  2.71 us (1%)
    all_gather x3, blocking collectives, entering(): gathered = jax.tree.map(lambda a: lax.all_gather(a, axis), part)  59.4 us
    dynamic_slice x128, local copies, waits for them, and re-layouts, local(): lax.scan(propagate_one_day, (leading_element, jnp.ones((driver_value_hist...  43 us
    mul x64, other arithmetic, propagate_one_day(): decay = decay * driver_value_now  40.6 us
    all_gather x1, waiting for transfers between devices, local(): lax.all_gather(correlation_mixer, 'paths', axis=0, tiled=True)  35.3 us
    all_gather x1, blocking collectives, summed_here(): parts = lax.all_gather(x, mesh_axis, axis=0, tiled=False)  17.5 us
    dynamic_update_slice x64, local copies, waits for them, and re-layouts, local(): lax.scan(propagate_one_day, (leading_element, jnp.ones((driver_value_hist...  7.04 us
  transfers between devices with their start and end apart: 1, of which 1 were waited for; matrix products, arithmetic and copies ran while one was open for 1% of the time, Pallas kernels for 0%

profile of v1, /device:TPU:0, one launch (start us, length us, event | category | flops | bytes accessed | tf_op | source)
XLA Modules:
  0.0 228.0 jit_solution(2958591011996473090)
XLA Ops:
  6.5 0.7 all-gather.8.cloned.1.call-update
  7.3 0.7 reshape.43
  8.0 0.7 negate_sqrt_fusion
  8.7 0.7 broadcast_select_fusion
  9.4 35.3 %all-gather.8.cloned.1.call-done = bf16[1024,1024]{1,0:T(8,128)(2,1)} async-done(((bf16[512,1024]{1,0:T(8,128)(2,1)}), bf16[1024,1024]{1,0:T(8,128)(2,1)}) %all-gather.8.cloned.1.call-update) | async-done | bytes 2097168 | tf_op jit(solution)/shard_map/all_gather | solution.py:40
  44.7 2.5 %fusion.2 = f32[64,4,1024]{2,0,1:T(8,128)S(1)} fusion(bf16[1024,1024]{1,0:T(8,128)(2,1)} %all-gather.8.cloned.1.call-done, bf16[64,4,1024]{2,1,0:T(4,128)(2,1)} %param.13), kind=kOutput, calls=%fused_computation.10 | convolution fusion | flops 536870912 | bytes 3670016 | tf_op jit(solution)/shard_map/spf,fg->spg/dot_general | solution.py:37
  47.2 95.1 %while.41 = (s32[]{:T(128)}, f32[4,1024]{1,0:T(4,128)S(1)}, f32[1024]{0:T(1024)S(1)}, f32[64,4,1024]{2,1,0:T(4,128)S(1)}, f32[64,1024]{1,0:T(8,128)S(1)}, /*inde...) while((s32[]{:T(128)}, f32[4,1024]{1,0:T(4,128)S(1)}, ...), condition=%wide.region_1.2_spmd.clone, body=%wide.region_0.1_spmd.clone.sunk | while | flops 15363 | bytes 131219 | solution.py:57
  47.3 0.7 dynamic_slice.37
  48.7 0.7 dynamic_slice.37
  50.2 0.7 dynamic_slice.37
  51.7 0.7 dynamic_slice.37
  53.2 0.7 dynamic_slice.37
  54.7 0.7 dynamic_slice.37
  56.2 0.7 dynamic_slice.37
  57.7 0.7 dynamic_slice.37
  59.1 0.7 dynamic_slice.37
  60.6 0.7 dynamic_slice.37
  62.1 0.7 dynamic_slice.37
  63.6 0.7 dynamic_slice.37
  65.1 0.7 dynamic_slice.37
  66.6 0.7 dynamic_slice.37
  68.1 0.7 dynamic_slice.37
  69.5 0.7 dynamic_slice.37
  71.0 0.7 dynamic_slice.37
  72.5 0.7 dynamic_slice.37
  74.0 0.7 dynamic_slice.37
  75.5 0.7 dynamic_slice.37
  77.0 0.7 dynamic_slice.37
  78.5 0.7 dynamic_slice.37
  79.9 0.7 dynamic_slice.37
  81.4 0.7 dynamic_slice.37
  82.9 0.7 dynamic_slice.37
  84.4 0.7 dynamic_slice.37
  85.9 0.7 dynamic_slice.37
  87.4 0.7 dynamic_slice.37
  88.9 0.7 dynamic_slice.37
  90.3 0.7 dynamic_slice.37
  91.8 0.7 dynamic_slice.37
  93.3 0.7 dynamic_slice.37
  94.8 0.7 dynamic_slice.37
  96.3 0.7 dynamic_slice.37
  97.8 0.7 dynamic_slice.37
  99.3 0.7 dynamic_slice.37
  100.7 0.7 dynamic_slice.37
  102.2 0.7 dynamic_slice.37
  103.7 0.7 dynamic_slice.37
  105.2 0.7 dynamic_slice.37
  106.7 0.7 dynamic_slice.37
  108.2 0.7 dynamic_slice.37
  109.7 0.7 dynamic_slice.37
  111.1 0.7 dynamic_slice.37
  112.6 0.7 dynamic_slice.37
  114.1 0.7 dynamic_slice.37
  115.6 0.7 dynamic_slice.37
  117.1 0.7 dynamic_slice.37
  118.6 0.7 dynamic_slice.37
  120.1 0.7 dynamic_slice.37
  121.5 0.7 dynamic_slice.37
  123.0 0.7 dynamic_slice.37
  124.5 0.7 dynamic_slice.37
  142.3 22.0 %all-gather.3 = f32[16,4,1024]{2,1,0:T(4,128)S(1)} all-gather(f32[1,4,1024]{2,1,0:T(4,128)S(1)} %bitcast.45), channel_id=3, replica_groups=mesh['paths'=2,'tm'=16] {'tm'}, dimensions={0}, use_global_device_ids=true | all-gather | bytes 278528 | tf_op jit(solution)/shard_map/all_gather | solution.py:15
  164.4 17.6 %all-gather = f32[16384]{0:T(1024)S(1)} all-gather(f32[1024]{0:T(1024)S(1)} %get-tuple-element.124), channel_id=2, replica_groups=mesh['paths'=2,'tm'=16] {'tm'}, dimensions={0}, use_global_device_ids=true | all-gather | bytes 69632 | tf_op jit(solution)/shard_map/all_gather | solution.py:15
  182.9 19.7 %all-gather.4 = f32[16,1,4]{2,1,0:T(1,128)S(1)} all-gather(f32[1,1,4]{2,1,0:T(1,128)S(1)} %slice_bitcast_fusion), channel_id=1, replica_groups=mesh['paths'=2,'tm'=16] {'tm'}, dimensions={0}, use_global_device_ids=true | all-gather | bytes 272 | tf_op jit(solution)/shard_map/all_gather | solution.py:15
  203.1 17.5 %all-gather.5 = f32[16,4,128]{2,1,0:T(4,128)S(1)} all-gather(f32[1,4,128]{2,1,0:T(4,128)S(1)} %multiply_bitcast_fusion), channel_id=4, replica_groups=mesh['paths'=2,'tm'=16] {'tm'}, dimensions={0}, use_global_device_ids=true | all-gather | bytes 34816 | tf_op jit(solution)/shard_map/all_gather | solution.py:8
  (291 shorter events, 59.9 us)
Async XLA Ops:
  6.5 196.2 %copy-start = (bf16[1024,128]{1,0:T(8,128)(2,1)S(1)}, bf16[1024,128]{1,0:T(8,128)(2,1)}, u32[]{:S(2)}) copy-start(bf16[1024,128]{1,0:T(8,128)(2,1)} %param.18) | copy-start | bytes 786436
  6.5 38.2 %all-gather.8.cloned.1.call-start = ((), (), s32[]{:S(2)}) async-start(), calls=%async_computation | async-start | bytes 3145728 | tf_op jit(solution)/shard_map/all_gather | solution.py:40
  7.3 40.0 %copy-start.1 = (f32[64]{0:T(128)S(1)}, f32[64]{0:T(128)}, u32[]{:S(2)}) copy-start(f32[64]{0:T(128)} %param.17) | copy-start | bytes 772
Sparse Core Ops, SparseCore 0:
  8.9 35.8 all-gather.7
